TPU v7x, 256 devices: a whole 4x4x8 slice. The times are simulated.
256 devices in a mesh: pool: 16 (over z, core), tensor: 16 (over y, x).
Axes of the slice: x: 4, y: 4, z: 8, core: 2. Of those that a mesh axis runs over, the one named last changes fastest.
Arguments:
- hidden: bfloat16 [8192, 14336], P('pool', 'tensor'), may hold values from -6 to 6
- down_weight: bfloat16 [14336, 8192], P('tensor', 'pool'), may hold values from -0.046875 to 0.046875
- adapter_shrink: bfloat16 [32, 14336, 64], P('pool', 'tensor'), may hold values from -0.046875 to 0.046875
- adapter_expand: bfloat16 [32, 8192, 64], P('pool', 'tensor'), may hold values from -0.75 to 0.75
- block_adapter: int32 [64], P('pool'), may hold values from 0 to 31, as said below
- block_rows: int32 [64], P('pool'), may hold values from 1 to 128, 6144 in all
Outputs:
- projected: bfloat16 [8192, 8192], P(('pool', 'tensor'))
Inputs may be any that keep to these rules, and one draw needn't show every extreme that they name: `block_adapter`: within each aligned run of 4 blocks (the rows of one pool index) no two blocks name adapters with the same a // 2. `block_rows`: some block is full.
All inputs are finite; a program needn't handle non-finite values.
Results may differ from a plain program's by a relative error of at most 0.02.
Values may be sent and summed in bfloat16 or wider, within the bound.
A program may use at most 128 MiB of HBM per device.

v0:
```python
import jax
import jax.numpy as jnp
from jax import lax
from jax.sharding import PartitionSpec as P

BLOCK = 128
adapter_scale_factor = 0.5


def shards(hidden, down_weight, adapter_shrink, adapter_expand, block_adapter, block_rows):
    input_rows, feat = hidden.shape
    block_count = block_adapter.shape[0]
    column_span = adapter_expand.shape[1]
    tensor_pos = lax.axis_index("tensor")
    tensor_count = lax.axis_size("tensor")
    own_rows = input_rows // tensor_count
    blocks = hidden.reshape(block_count, BLOCK, feat)
    partial_value = jnp.dot(
        hidden,
        lax.all_gather(down_weight, "pool", axis=1, tiled=True),
        preferred_element_type=jnp.float32,
    )
    total = lax.psum_scatter(
        partial_value.astype(jnp.bfloat16), "tensor", scatter_dimension=0, tiled=True
    ).astype(jnp.float32)
    shrink_piece = lax.all_gather(adapter_shrink, "pool", axis=0, tiled=True)
    expand_piece = lax.all_gather(adapter_expand, "pool", axis=0, tiled=True)
    idents = jnp.arange(shrink_piece.shape[0], dtype=jnp.int32)
    pick = (block_adapter[:, None] == idents[None, :]).astype(jnp.bfloat16)
    first = jnp.einsum("bk,kfr->bfr", pick, shrink_piece, preferred_element_type=jnp.float32)
    second = jnp.einsum("bk,kcr->bcr", pick, expand_piece, preferred_element_type=jnp.float32)
    shrink = jnp.einsum(
        "bnf,bfr->bnr", blocks, first.astype(jnp.bfloat16), preferred_element_type=jnp.float32
    )
    summed_shrink = lax.psum(shrink.astype(jnp.bfloat16), "tensor")
    enlarged_rows = jnp.einsum(
        "bnr,bcr->bnc",
        summed_shrink,
        second.astype(jnp.bfloat16),
        preferred_element_type=jnp.float32,
    )
    adapter_delta_columns = (
        (adapter_scale_factor * enlarged_rows).astype(jnp.bfloat16).reshape(input_rows, column_span)
    )
    delta_mine = lax.all_to_all(
        adapter_delta_columns, "tensor", split_axis=0, concat_axis=1, tiled=True
    )
    total = total + delta_mine.astype(jnp.float32)
    row_ids = tensor_pos * own_rows + jnp.arange(own_rows, dtype=jnp.int32)
    owning = (row_ids // BLOCK)[:, None] == jnp.arange(block_count, dtype=jnp.int32)[None, :]
    lengths = jnp.sum(jnp.where(owning, block_rows[None, :], 0), axis=1)
    valid = (row_ids % BLOCK < lengths).astype(jnp.float32)
    return (total * valid[:, None]).astype(jnp.bfloat16)


def solution(mesh):
    in_specs = (
        P("pool", "tensor"),
        P("tensor", "pool"),
        P("pool", "tensor", None),
        P("pool", "tensor", None),
        P("pool"),
        P("pool"),
    )
    out_specs = P(("pool", "tensor"), None)
    return jax.shard_map(shards, mesh=mesh, in_specs=in_specs, out_specs=out_specs, check_vma=False)
```

profile of v0, /device:TPU:2, one launch (start us, length us, event | category | flops | bytes accessed | tf_op | source)
XLA Modules:
  0.0 374.3 jit_solution(14904361085306204502)
XLA Ops:
  6.5 0.0 copy-start
  6.5 0.0 all-gather.6.cloned.1.call-start
  6.5 0.7 all-gather.6.cloned.1.call-update
  7.3 0.0 all-gather.4.cloned.1.call-start
  7.3 0.7 all-gather.4.cloned.1.call-update
  8.0 0.0 all-gather.8.cloned.1.call-start
  8.1 0.7 all-gather.8.cloned.1.call-update
  8.7 0.0 all-reduce.2.cloned.1.call-start
  8.8 45.0 %all-gather.6.cloned.1.call-done = bf16[32,896,64]{1,2,0:T(8,128)(2,1)} async-done(((bf16[2,896,64]{1,2,0:T(8,128)(2,1)}), bf16[32,896,64]{1,2,0:T(8,128)(2,1)}) %all-gather.6.cloned.1.call-update) | async-done | bytes 3670032 | tf_op jit(solution)/shard_map/all_gather | solution.py:26
  53.8 5.0 %fusion.5 = bf16[4,896,64]{1,0,2:T(4,128)(2,1)S(1)} fusion(bf16[32,896,64]{1,2,0:T(8,128)(2,1)} %all-gather.6.cloned.1.call-done, s32[4]{0:T(128)} %param.10), kind=kOutput, calls=%fused_computation.7 | convolution fusion | flops 14909568 | bytes 4128784 | tf_op jit(solution)/shard_map/bk,kfr->bfr/dot_general | solution.py:30
  58.8 0.0 copy-done
  58.8 1.1 fusion.11
  59.9 0.0 all-reduce.2.cloned.1.call-update
  59.9 0.0 reduce-scatter.2.cloned.1.call-start
  59.9 79.8 %all-gather.4.cloned.1.call-done = bf16[896,8192]{1,0:T(8,128)(2,1)} async-done(((bf16[896,512]{1,0:T(8,128)(2,1)}), bf16[896,8192]{1,0:T(8,128)(2,1)}) %all-gather.4.cloned.1.call-update) | async-done | bytes 14680080 | tf_op jit(solution)/shard_map/all_gather | solution.py:20
  139.8 16.5 %convolution_convert_fusion = bf16[512,8192]{1,0:T(8,128)(2,1)} fusion(bf16[512,896]{1,0:T(8,128)(2,1)S(1)} %copy-done, bf16[896,8192]{1,0:T(8,128)(2,1)} %all-gather.4.cloned.1.call-done), kind=kOutput, calls=%fused_computation | convolution fusion | flops 7520387072 | bytes 23986176 | tf_op jit(solution)/shard_map/dot_general | solution.py:18
  156.3 0.0 copy-start.1
  156.3 0.0 reduce-scatter.2.cloned.1.call-update
  156.3 0.0 copy-start.2
  156.3 23.6 %all-gather.8.cloned.1.call-done = bf16[32,512,64]{1,2,0:T(8,128)(2,1)} async-done(((bf16[2,512,64]{1,2,0:T(8,128)(2,1)}), bf16[32,512,64]{1,2,0:T(8,128)(2,1)}) %all-gather.8.cloned.1.call-update) | async-done | bytes 2097168 | tf_op jit(solution)/shard_map/all_gather | solution.py:27
  179.9 0.0 copy-done.1
  179.9 2.9 fusion.8
  182.8 89.2 %all-reduce.2.cloned.1.call-done = bf16[4,128,64]{1,2,0:T(8,128)(2,1)} async-done(((bf16[4,128,64]{1,2,0:T(8,128)(2,1)}), bf16[4,128,64]{1,2,0:T(8,128)(2,1)}) %all-reduce.2.cloned.1.call-update) | async-done | bytes 65552 | tf_op jit(solution)/shard_map/psum | solution.py:35
  272.0 2.0 fusion.4
  274.0 5.7 %all-to-all-start = ((bf16[16,32,512]{2,1,0:T(8,128)(2,1)}), bf16[16,32,512]{2,1,0:T(8,128)(2,1)S(1)}, u32[]{:S(2)}, u32[]{:S(2)}) async-start(bf16[16,32,512]{2,1,0:T(8,128)(2,1)} %bitcast.3), calls=%async_computation.1 | async-start | bytes 1048576 | tf_op jit(solution)/shard_map/all_to_all | solution.py:45
  279.7 0.0 copy-done.2
  279.8 0.1 select_reduce_fusion
  279.9 8.6 %all-to-all-done = bf16[16,32,512]{2,1,0:T(8,128)(2,1)S(1)} async-done(((bf16[16,32,512]{2,1,0:T(8,128)(2,1)}), bf16[16,32,512]{2,1,0:T(8,128)(2,1)S(1)}, u32[]{:S(2)}, u32[]{:S(2)}) %all-to-all-start) | async-done | bytes 524320 | tf_op jit(solution)/shard_map/all_to_all | solution.py:45
  288.5 0.1 convert_bitcast_fusion
  288.6 0.1 copy.14
  288.7 77.0 %reduce-scatter.2.cloned.1.call-done = bf16[32,8192]{1,0:T(8,128)(2,1)} async-done(((bf16[512,8192]{1,0:T(8,128)(2,1)}), bf16[32,8192]{1,0:T(8,128)(2,1)}) %reduce-scatter.2.cloned.1.call-update) | async-done | bytes 524304 | tf_op jit(solution)/shard_map/reduce_scatter | solution.py:23
  365.7 2.0 multiply_convert_fusion
  (2 shorter events, 0.0 us)
Async XLA Ops:
  6.5 52.2 %copy-start = (bf16[512,896]{1,0:T(8,128)(2,1)S(1)}, bf16[512,896]{1,0:T(8,128)(2,1)}, u32[]{:S(2)}) copy-start(bf16[512,896]{1,0:T(8,128)(2,1)} %param.6) | copy-start | bytes 2752516
  6.5 47.2 %all-gather.6.cloned.1.call-start = ((), (), s32[]{:S(2)}) async-start(), calls=%async_computation.4 | async-start | bytes 3899392 | tf_op jit(solution)/shard_map/all_gather | solution.py:26
  7.3 132.5 %all-gather.4.cloned.1.call-start = ((), (), s32[]{:S(2)}) async-start(), calls=%async_computation.2 | async-start | bytes 15597568 | tf_op jit(solution)/shard_map/all_gather | solution.py:20
  8.0 171.9 %all-gather.8.cloned.1.call-start = ((), (), s32[]{:S(2)}) async-start(), calls=%async_computation.6 | async-start | bytes 2228224 | tf_op jit(solution)/shard_map/all_gather | solution.py:27
  8.7 263.3 %all-reduce.2.cloned.1.call-start = ((), (), s32[]{:S(2)}) async-start(), calls=%async_computation.5 | async-start | bytes 131072 | tf_op jit(solution)/shard_map/psum | solution.py:35
  59.9 305.8 %reduce-scatter.2.cloned.1.call-start = ((), (), s32[]{:S(2)}) async-start(), calls=%async_computation.3 | async-start | bytes 8912896 | tf_op jit(solution)/shard_map/reduce_scatter | solution.py:23
  156.3 23.6 %copy-start.1 = (s32[4]{0:T(128)S(1)}, s32[4]{0:T(128)}, u32[]{:S(2)}) copy-start(s32[4]{0:T(128)} %param.10) | copy-start | bytes 52
  156.3 123.4 %copy-start.2 = (s32[4]{0:T(128)S(1)}, s32[4]{0:T(128)}, u32[]{:S(2)}) copy-start(s32[4]{0:T(128)} %param.11) | copy-start | bytes 52
  274.0 14.5 %all-to-all-start = ((bf16[16,32,512]{2,1,0:T(8,128)(2,1)}), bf16[16,32,512]{2,1,0:T(8,128)(2,1)S(1)}, u32[]{:S(2)}, u32[]{:S(2)}) async-start(bf16[16,32,512]{2,1,0:T(8,128)(2,1)} %bitcast.3), calls=%async_computation.1 | async-start | bytes 1048576 | tf_op jit(solution)/shard_map/all_to_all | solution.py:45
Sparse Core Ops, SparseCore 0:
  9.2 44.5 all-gather.5
  55.6 84.1 all-gather.3
  141.6 38.2 all-gather.7
  183.0 89.0 all-reduce.1
  276.0 89.6 reduce-scatter.1
where the time goes:
time: 375 us; the launch traced here: 374 us
  waiting for transfers between devices  325 us (87%)
  matrix products  27.4 us (7%)
  between operations  13.2 us (4%)
  starting transfers between devices  5.89 us (2%)
    psum x1, waiting for transfers between devices, shards(): summed_shrink = lax.psum(shrink.astype(jnp.bfloat16), 'tensor')  89.2 us
    all_gather x1, waiting for transfers between devices, shards(): lax.all_gather(down_weight, 'pool', axis=1, tiled=True)  79.8 us
    reduce_scatter x1, waiting for transfers between devices, shards(): lax.psum_scatter(partial_value.astype(jnp.bfloat16), 'tensor', scatter_di...  77 us
    all_gather x1, waiting for transfers between devices, shards(): shrink_piece = lax.all_gather(adapter_shrink, 'pool', axis=0, tiled=True)  45 us
    all_gather x1, waiting for transfers between devices, shards(): expand_piece = lax.all_gather(adapter_expand, 'pool', axis=0, tiled=True)  23.6 us
    dot_general x1, matrix products, shards(): jnp.dot(hidden, lax.all_gather(down_weight, 'pool', axis=1, tiled=True),...  16.5 us
    all_to_all x1, waiting for transfers between devices, shards(): lax.all_to_all(adapter_delta_columns, 'tensor', split_axis=0, concat_axis...  8.61 us
  transfers between devices with their start and end apart: 6, of which 6 were waited for; matrix products, arithmetic and copies ran while one was open for 7% of the time, Pallas kernels for 0%

commit v1 on v0

--- a/solution.py
+++ b/solution.py
@@ -23,7 +23,9 @@
     total = lax.psum_scatter(
         partial_value.astype(jnp.bfloat16), "tensor", scatter_dimension=0, tiled=True
     ).astype(jnp.float32)
-    shrink_piece = lax.all_gather(adapter_shrink, "pool", axis=0, tiled=True)
+    shrink_piece = jnp.concatenate(
+        lax.all_to_all(jnp.stack([adapter_shrink] * lax.axis_size("pool")), "pool", 0, 0), axis=0
+    )
     expand_piece = lax.all_gather(adapter_expand, "pool", axis=0, tiled=True)
     idents = jnp.arange(shrink_piece.shape[0], dtype=jnp.int32)
     pick = (block_adapter[:, None] == idents[None, :]).astype(jnp.bfloat16)

time: 375 us -> 340 us (0.907)
  waiting for transfers between devices: 325 us -> 277 us
  starting transfers between devices: 5.89 us -> 14.6 us
    all_to_all x0 -> x1, waiting for transfers between devices: none -> 118 us  [shards(): lax.all_to_all(jnp.stack([adapter_shrink] * lax.axis_size('pool')), 'pool...]
    psum x1, waiting for transfers between devices: 89.2 us -> 18.8 us  [shards(): summed_shrink = lax.psum(shrink.astype(jnp.bfloat16), 'tensor')]
    all_gather x1, waiting for transfers between devices: 79.8 us -> 28.1 us  [shards(): lax.all_gather(down_weight, 'pool', axis=1, tiled=True)]
    all_gather x1 -> x0, waiting for transfers between devices: 45 us -> none  [shards(): shrink_piece = lax.all_gather(adapter_shrink, 'pool', axis=0, tiled=True)]
    all_to_all x0 -> x1, starting transfers between devices: none -> 8.75 us  [shards(): lax.all_to_all(jnp.stack([adapter_shrink] * lax.axis_size('pool')), 'pool...]
  transfers between devices with their start and end apart: 6 -> 6, of which waited for: 6 -> 6; matrix products, arithmetic and copies ran while one was open for 7% -> 9% of each run, Pallas kernels for 0% -> 0%
where the time goes in v1:
time: 340 us
  waiting for transfers between devices  277 us (81%)
  matrix products  27.5 us (8%)
  between operations  14.9 us (4%)
  starting transfers between devices  14.6 us (4%)
    all_to_all x1, waiting for transfers between devices, shards(): lax.all_to_all(jnp.stack([adapter_shrink] * lax.axis_size('pool')), 'pool...  118 us
    reduce_scatter x1, waiting for transfers between devices, shards(): lax.psum_scatter(partial_value.astype(jnp.bfloat16), 'tensor', scatter_di...  77.3 us
    all_gather x1, waiting for transfers between devices, shards(): lax.all_gather(down_weight, 'pool', axis=1, tiled=True)  28.1 us
    all_gather x1, waiting for transfers between devices, shards(): expand_piece = lax.all_gather(adapter_expand, 'pool', axis=0, tiled=True)  24.4 us
    psum x1, waiting for transfers between devices, shards(): summed_shrink = lax.psum(shrink.astype(jnp.bfloat16), 'tensor')  18.8 us
    dot_general x1, matrix products, shards(): jnp.dot(hidden, lax.all_gather(down_weight, 'pool', axis=1, tiled=True),...  16.5 us
    all_to_all x1, starting transfers between devices, shards(): lax.all_to_all(jnp.stack([adapter_shrink] * lax.axis_size('pool')), 'pool...  8.75 us
    all_to_all x1, waiting for transfers between devices, shards(): lax.all_to_all(adapter_delta_columns, 'tensor', split_axis=0, concat_axis...  8.61 us
  transfers between devices with their start and end apart: 6, of which 6 were waited for; matrix products, arithmetic and copies ran while one was open for 9% of the time, Pallas kernels for 0%

profile of v1, /device:TPU:2, one launch (start us, length us, event | category | flops | bytes accessed | tf_op | source)
XLA Modules:
  0.0 339.6 jit_solution(8874728989844227881)
XLA Ops:
  7.4 0.0 copy-start
  7.4 0.0 all-gather.3.cloned.1.call-start
  7.4 0.7 all-gather.3.cloned.1.call-update
  8.1 3.3 stack.2
  11.4 0.0 copy-start.1
  11.4 8.7 %all-to-all-start = ((bf16[16,2,896,64]{2,3,1,0:T(8,128)(2,1)}), bf16[16,2,896,64]{2,3,1,0:T(8,128)(2,1)}, u32[]{:S(2)}, u32[]{:S(2)}) async-start(bf16[16,2,896,64]{2,3,1,0:T(8,128)(2,1)} %stack.2), calls=%async_computation.1 | async-start | bytes 7340032 | tf_op jit(solution)/shard_map/all_to_all | solution.py:27
  20.1 0.0 all-gather.5.cloned.1.call-start
  20.2 0.7 all-gather.5.cloned.1.call-update
  20.9 0.0 all-reduce.2.cloned.1.call-start
  20.9 118.4 %all-to-all-done = bf16[16,2,896,64]{2,3,1,0:T(8,128)(2,1)} async-done(((bf16[16,2,896,64]{2,3,1,0:T(8,128)(2,1)}), bf16[16,2,896,64]{2,3,1,0:T(8,128)(2,1)}, u32[]{:S(2)}, u32[]{:S(2)}) %all-to-all-start) | async-done | bytes 3670048 | tf_op jit(solution)/shard_map/all_to_all | solution.py:27
  139.4 0.0 copy-done.1
  139.4 5.1 %fusion.5 = bf16[4,896,64]{1,0,2:T(4,128)(2,1)S(1)} fusion(bf16[32,896,64]{1,2,0:T(8,128)(2,1)} %bitcast.1, s32[4]{0:T(128)S(1)} %copy-done.1), kind=kOutput, calls=%fused_computation.7 | convolution fusion | flops 14909568 | bytes 4128784 | tf_op jit(solution)/shard_map/bk,kfr->bfr/dot_general | solution.py:32
  144.5 0.0 copy-done
  144.5 1.1 fusion.11
  145.6 0.0 all-reduce.2.cloned.1.call-update
  145.6 0.0 reduce-scatter.2.cloned.1.call-start
  145.6 28.1 %all-gather.3.cloned.1.call-done = bf16[896,8192]{1,0:T(8,128)(2,1)} async-done(((bf16[896,512]{1,0:T(8,128)(2,1)}), bf16[896,8192]{1,0:T(8,128)(2,1)}) %all-gather.3.cloned.1.call-update) | async-done | bytes 14680080 | tf_op jit(solution)/shard_map/all_gather | solution.py:20
  173.7 16.5 %convolution_convert_fusion = bf16[512,8192]{1,0:T(8,128)(2,1)} fusion(bf16[512,896]{1,0:T(8,128)(2,1)S(1)} %copy-done, bf16[896,8192]{1,0:T(8,128)(2,1)} %all-gather.3.cloned.1.call-done), kind=kOutput, calls=%fused_computation | convolution fusion | flops 7520387072 | bytes 23986176 | tf_op jit(solution)/shard_map/dot_general | solution.py:18
  190.2 0.0 reduce-scatter.2.cloned.1.call-update
  190.3 0.0 copy-start.2
  190.3 24.4 %all-gather.5.cloned.1.call-done = bf16[32,512,64]{1,2,0:T(8,128)(2,1)} async-done(((bf16[2,512,64]{1,2,0:T(8,128)(2,1)}), bf16[32,512,64]{1,2,0:T(8,128)(2,1)}) %all-gather.5.cloned.1.call-update) | async-done | bytes 2097168 | tf_op jit(solution)/shard_map/all_gather | solution.py:29
  214.6 2.9 fusion.8
  217.5 18.8 %all-reduce.2.cloned.1.call-done = bf16[4,128,64]{1,2,0:T(8,128)(2,1)} async-done(((bf16[4,128,64]{1,2,0:T(8,128)(2,1)}), bf16[4,128,64]{1,2,0:T(8,128)(2,1)}) %all-reduce.2.cloned.1.call-update) | async-done | bytes 65552 | tf_op jit(solution)/shard_map/psum | solution.py:37
  236.3 2.0 fusion.4
  238.2 5.7 %all-to-all-start.1 = ((bf16[16,32,512]{2,1,0:T(8,128)(2,1)}), bf16[16,32,512]{2,1,0:T(8,128)(2,1)S(1)}, u32[]{:S(2)}, u32[]{:S(2)}) async-start(bf16[16,32,512]{2,1,0:T(8,128)(2,1)} %bitcast.4), calls=%async_computation.2 | async-start | bytes 1048576 | tf_op jit(solution)/shard_map/all_to_all | solution.py:47
  244.0 0.0 copy-done.2
  244.0 0.1 select_reduce_fusion
  244.1 8.6 %all-to-all-done.1 = bf16[16,32,512]{2,1,0:T(8,128)(2,1)S(1)} async-done(((bf16[16,32,512]{2,1,0:T(8,128)(2,1)}), bf16[16,32,512]{2,1,0:T(8,128)(2,1)S(1)}, u32[]{:S(2)}, u32[]{:S(2)}) %all-to-all-start.1) | async-done | bytes 524320 | tf_op jit(solution)/shard_map/all_to_all | solution.py:47
  252.7 0.1 convert_bitcast_fusion
  252.8 0.1 copy.16
  252.9 77.3 %reduce-scatter.2.cloned.1.call-done = bf16[32,8192]{1,0:T(8,128)(2,1)} async-done(((bf16[512,8192]{1,0:T(8,128)(2,1)}), bf16[32,8192]{1,0:T(8,128)(2,1)}) %reduce-scatter.2.cloned.1.call-update) | async-done | bytes 524304 | tf_op jit(solution)/shard_map/reduce_scatter | solution.py:23
  330.2 2.0 multiply_convert_fusion
  (2 shorter events, 0.0 us)
Async XLA Ops:
  7.4 137.1 %copy-start = (bf16[512,896]{1,0:T(8,128)(2,1)S(1)}, bf16[512,896]{1,0:T(8,128)(2,1)}, u32[]{:S(2)}) copy-start(bf16[512,896]{1,0:T(8,128)(2,1)} %param.6) | copy-start | bytes 2752516
  7.4 166.4 %all-gather.3.cloned.1.call-start = ((), (), s32[]{:S(2)}) async-start(), calls=%async_computation.3 | async-start | bytes 15597568 | tf_op jit(solution)/shard_map/all_gather | solution.py:20
  11.4 128.0 %copy-start.1 = (s32[4]{0:T(128)S(1)}, s32[4]{0:T(128)}, u32[]{:S(2)}) copy-start(s32[4]{0:T(128)} %param.10) | copy-start | bytes 52
  11.4 128.0 %all-to-all-start = ((bf16[16,2,896,64]{2,3,1,0:T(8,128)(2,1)}), bf16[16,2,896,64]{2,3,1,0:T(8,128)(2,1)}, u32[]{:S(2)}, u32[]{:S(2)}) async-start(bf16[16,2,896,64]{2,3,1,0:T(8,128)(2,1)} %stack.2), calls=%async_computation.1 | async-start | bytes 7340032 | tf_op jit(solution)/shard_map/all_to_all | solution.py:27
  20.1 194.5 %all-gather.5.cloned.1.call-start = ((), (), s32[]{:S(2)}) async-start(), calls=%async_computation.6 | async-start | bytes 2228224 | tf_op jit(solution)/shard_map/all_gather | solution.py:29
  20.9 215.4 %all-reduce.2.cloned.1.call-start = ((), (), s32[]{:S(2)}) async-start(), calls=%async_computation.5 | async-start | bytes 131072 | tf_op jit(solution)/shard_map/psum | solution.py:37
  145.6 184.6 %reduce-scatter.2.cloned.1.call-start = ((), (), s32[]{:S(2)}) async-start(), calls=%async_computation.4 | async-start | bytes 8912896 | tf_op jit(solution)/shard_map/reduce_scatter | solution.py:23
  190.3 53.7 %copy-start.2 = (s32[4]{0:T(128)S(1)}, s32[4]{0:T(128)}, u32[]{:S(2)}) copy-start(s32[4]{0:T(128)} %param.11) | copy-start | bytes 52
  238.2 14.5 %all-to-all-start.1 = ((bf16[16,32,512]{2,1,0:T(8,128)(2,1)}), bf16[16,32,512]{2,1,0:T(8,128)(2,1)S(1)}, u32[]{:S(2)}, u32[]{:S(2)}) async-start(bf16[16,32,512]{2,1,0:T(8,128)(2,1)} %bitcast.4), calls=%async_computation.2 | async-start | bytes 1048576 | tf_op jit(solution)/shard_map/all_to_all | solution.py:47
Sparse Core Ops, SparseCore 0:
  10.2 163.5 all-gather.2
  175.7 38.8 all-gather.4
Sparse Core Ops, SparseCore 1:
  145.7 90.5 all-reduce.1
  240.3 89.8 reduce-scatter.1
